TPU v7x, 256 devices: a whole 4x4x8 slice. The times are simulated.
256 devices in a mesh: blk: 16 (over y, x_lo, core), rep: 16 (over z, x_hi).
Axes of the slice: x: 4 (x_hi: 2, x_lo: 2; x = x_hi * 2 + x_lo), y: 4, z: 8, core: 2. Of those that a mesh axis runs over, the one named last changes fastest.
Arguments:
- features: bfloat16 [65536, 128], P(('blk', 'rep')), may hold values from -6 to 6
- edge_rows: int32 [16, 16, 32, 256], P('blk', None, 'rep'), may hold values from 0 to 4095
- edge_cols: int32 [16, 16, 32, 256], P('blk', None, 'rep'), may hold values from 0 to 127
- weight: bfloat16 [128, 256], replicated, may hold values from -0.5 to 0.5
- bias: float32 [256], replicated, may hold values from -3 to 3
- upstream: bfloat16 [65536, 256], P('blk'), may hold values from -6 to 6
- train_mask: int32 [65536], P('blk'), may hold values 0 or 1
Outputs:
- activations: bfloat16 [65536, 256], P(('blk', 'rep'))
- grad_features: bfloat16 [65536, 128], P(('blk', 'rep'))
- grad_weight: float32 [128, 256], replicated
- grad_bias: float32 [256], replicated
Inputs may be any that keep to these rules, and one draw needn't show every extreme that they name: `edge_rows`: target indices within a panel. `edge_cols`: source indices within a column block.
All inputs are finite; a program needn't handle non-finite values. No bound on the sum of `train_mask` on one device may be relied on, other than what follows from the above.
Results may differ from a plain program's by a relative error of at most 0.018.
Values may be sent and summed in bfloat16 or wider, within the bound.
No kernel may reach another device: no remote copies, remote signals or barrier semaphores. Data moves between devices by JAX's collectives and lax.ppermute only.
A program may use at most 64 MiB of HBM per device.

v0:
```python
import math
import jax
import jax.numpy as jnp
from jax import lax
from jax.sharding import PartitionSpec as P

CB = 128


def from_everyone(value, axis):
    copies = jnp.broadcast_to(value, (lax.axis_size(axis), *value.shape))
    return lax.all_to_all(copies, axis, split_axis=0, concat_axis=0, tiled=True)


def in_order(parts, dim):
    lengths = list(parts.shape[1:])
    lengths[dim] *= parts.shape[0]
    return jnp.moveaxis(parts, 0, dim).reshape(lengths)


def gathered_copies(value, axis, dim):
    parts = from_everyone(value, axis)
    return in_order(parts, dim)


def in_blocks(value, dim, count):
    lengths = value.shape
    parts = value.reshape(*lengths[:dim], count, lengths[dim] // count, *lengths[dim + 1 :])
    return jnp.moveaxis(parts, dim, 0)


def summed_on_arrival(value, axis, dim):
    parts = in_blocks(value, dim, lax.axis_size(axis))
    arrived = lax.all_to_all(parts, axis, split_axis=0, concat_axis=0, tiled=True)
    return arrived.astype(jnp.float32).sum(axis=0)


def sent_together(arrays, axis, dim, along):
    widths = [math.prod(a.shape[along:]) for a in arrays]
    both = jnp.concatenate(
        [a.reshape(*a.shape[:along], w) for a, w in zip(arrays, widths)], axis=along
    )
    whole = summed_on_arrival(both, axis, dim)
    parts = jnp.split(whole, [sum(widths[:k]) for k in range(1, len(widths))], axis=along)
    return tuple((b.reshape(*whole.shape[:along], *a.shape[along:]) for a, b in zip(arrays, parts)))


def together(arrays, axis):
    ends = [0]
    for a in arrays:
        ends.append(ends[-1] + a.size)
    subtotal = lax.psum(jnp.concatenate([a.ravel() for a in arrays]), axis)
    return tuple((subtotal[b:e].reshape(a.shape) for a, b, e in zip(arrays, ends, ends[1:])))


def dense_layer(feats, gathered, counts, upstream, train_mask, weight, bias):
    degree = 1.0 + counts
    mixed_in = ((feats.astype(jnp.float32) + gathered) / degree[:, None]).astype(jnp.bfloat16)
    pre_act = jnp.dot(mixed_in, weight, preferred_element_type=jnp.float32) + bias
    gate_value = jax.nn.sigmoid(pre_act)
    activations = (pre_act * gate_value).astype(jnp.bfloat16)
    slope = gate_value * (1.0 + pre_act * (1.0 - gate_value))
    grad_pre = (
        upstream.astype(jnp.float32) * train_mask.astype(jnp.float32)[:, None] * slope
    ).astype(jnp.bfloat16)
    scaled_back = (
        jnp.dot(grad_pre, weight.T, preferred_element_type=jnp.float32) / degree[:, None]
    ).astype(jnp.bfloat16)
    return (mixed_in, activations, grad_pre, scaled_back)


def on_device(features, edge_rows, edge_cols, weight, bias, upstream, train_mask):
    piece_rows, feature_width = features.shape
    edge_slots = edge_rows.shape[-1]
    panel_rows = upstream.shape[0]
    flat_rows = edge_rows.reshape(-1, edge_slots)
    flat_cols = edge_cols.reshape(-1, edge_slots)
    rep_index = lax.axis_index("rep")
    counts_part = jnp.zeros((panel_rows,), jnp.float32).at[flat_rows.reshape(-1)].add(1.0)
    shard_rows = gathered_copies(features, "blk", 0)
    block_count = shard_rows.shape[0] // CB
    targets = flat_rows
    columns = flat_cols
    offsets = (jnp.arange(block_count, dtype=jnp.int32) * CB)[:, None]
    values = jnp.take(shard_rows, (offsets + columns).reshape(-1), axis=0).astype(jnp.float32)
    partial_sums = (
        jnp.zeros((panel_rows, feature_width), jnp.float32).at[targets.reshape(-1)].add(values)
    )
    gathered, counts = sent_together(
        (partial_sums.astype(jnp.bfloat16), counts_part.astype(jnp.bfloat16)), "rep", 0, 1
    )
    own_upstream = lax.dynamic_slice_in_dim(upstream, rep_index * piece_rows, piece_rows, 0)
    own_mask = lax.dynamic_slice_in_dim(train_mask, rep_index * piece_rows, piece_rows, 0)
    mixed_own, activations, grad_own, back_own = dense_layer(
        features, gathered, counts, own_upstream, own_mask, weight, bias
    )
    back_panel = gathered_copies(back_own, "rep", 0)
    weight_part = lax.dot_general(
        mixed_own, grad_own, (((0,), (0,)), ((), ())), preferred_element_type=jnp.float32
    )
    bias_part = jnp.sum(grad_own.astype(jnp.float32), axis=0)
    grad_weight, grad_bias = together((weight_part, bias_part), ("blk", "rep"))
    row_count = piece_rows * lax.axis_size("blk")
    block_count = row_count // CB
    targets = flat_rows
    columns = flat_cols
    values = jnp.take(back_panel, targets.reshape(-1), axis=0).reshape(
        block_count, edge_slots, feature_width
    )
    one_hot = (columns[:, :, None] == jnp.arange(CB, dtype=jnp.int32)[None, None, :]).astype(
        jnp.bfloat16
    )
    block_terms = jnp.einsum("nec,ned->ncd", one_hot, values, preferred_element_type=jnp.float32)
    received = summed_on_arrival(
        block_terms.reshape(row_count, feature_width).astype(jnp.bfloat16), "blk", 0
    )
    grad_features = (back_own.astype(jnp.float32) + received).astype(jnp.bfloat16)
    return (activations, grad_features, grad_weight, grad_bias)


def solution(mesh):
    return jax.shard_map(
        on_device,
        mesh=mesh,
        in_specs=(
            P(("blk", "rep"), None),
            P("blk", None, "rep", None),
            P("blk", None, "rep", None),
            P(),
            P(),
            P("blk", None),
            P("blk"),
        ),
        out_specs=(P(("blk", "rep"), None), P(("blk", "rep"), None), P(), P()),
        check_vma=False,
    )
```

profile of v0, /device:TPU:1, one launch (start us, length us, event | category | flops | bytes accessed | tf_op | source)
XLA Modules:
  0.0 513.4 jit_solution(3568390661544370196)
XLA Ops:
  7.2 2.1 broadcast_in_dim.33
  9.3 6.9 %all-to-all-start = ((bf16[16,256,128]{2,1,0:T(8,128)(2,1)}), bf16[16,256,128]{2,1,0:T(8,128)(2,1)S(1)}, u32[]{:S(2)}, u32[]{:S(2)}) async-start(bf16[16,256,128]{2,1,0:T(8,128)(2,1)} %broadcast_in_dim.33), calls=%async_computation | async-start | bytes 2097152 | tf_op jit(solution)/shard_map/all_to_all | solution.py:12
  16.5 43.2 %scatter_custom_fusion.1 = f32[4096]{0:T(1024)S(1)} fusion(s32[8192]{0:T(1024)S(1)} %bitcast.37, f32[8192]{0:T(1024)S(1)} %broadcast.37, f32[]{:T(128)} %constant.15.clone.1), kind=kCustom, calls=%fused_computation.37 | custom fusion | flops 8192 | bytes 16388 | tf_op jit(solution)/shard_map/scatter-add | solution.py:79
  59.7 3.1 concatenate.15
  62.9 73.9 %scatter_custom_fusion = f32[4096,128]{1,0:T(8,128)S(1)} fusion(s32[8192]{0:T(1024)S(1)} %bitcast.38, pred[8192]{0:T(1024)(128)(4,1)S(1)} %compare_and_fusion.1, bf16[]{:T(256)} %constant.11.clone.2, f32[]{:T(128)} %constant.15.clone.1, bf16[4096,128]{1,0:T(8,128)(2,1)S(1)} %bitcast.25, s32[8192]{0:T(1024)S(1)} %broadcast_clamp_fusion), kind=kCustom, calls=%fused_computation.5 | custom fusion | flops 3145728 | bytes 3186694 | tf_op jit(solution)/shard_map/scatter-add | solution.py:87
  136.8 0.1 convert_element_type.55
  136.9 1.1 copy-done.1
  138.0 0.5 pad_maximum_fusion
  138.4 2.2 copy.16
  140.6 10.6 %all-to-all-start.1 = ((bf16[16,256,129]{1,2,0:T(8,128)(2,1)}), bf16[16,256,129]{1,2,0:T(8,128)(2,1)S(1)}, u32[]{:S(2)}, u32[]{:S(2)}) async-start(bf16[16,256,129]{1,2,0:T(8,128)(2,1)} %copy.16), calls=%async_computation.1 | async-start | bytes 2228224 | tf_op jit(solution)/shard_map/all_to_all | solution.py:34
  151.2 0.8 dynamic-slice_convert_fusion
  152.0 27.8 %all-to-all-done.1 = bf16[16,256,129]{1,2,0:T(8,128)(2,1)S(1)} async-done(((bf16[16,256,129]{1,2,0:T(8,128)(2,1)}), bf16[16,256,129]{1,2,0:T(8,128)(2,1)S(1)}, u32[]{:S(2)}, u32[]{:S(2)}) %all-to-all-start.1) | async-done | bytes 1056800 | tf_op jit(solution)/shard_map/all_to_all | solution.py:34
  179.8 0.2 convert_reduce_fusion
  180.1 0.1 divide_convert_fusion
  180.2 1.8 convert_reduce_fusion.2
  182.1 0.2 fusion.7
  182.3 1.2 broadcast_in_dim.36
  183.4 6.0 %all-to-all-start.2 = ((bf16[16,256,128]{2,1,0:T(8,128)(2,1)}), bf16[16,256,128]{2,1,0:T(8,128)(2,1)S(1)}, u32[]{:S(2)}, u32[]{:S(2)}) async-start(bf16[16,256,128]{2,1,0:T(8,128)(2,1)} %broadcast_in_dim.36), calls=%async_computation.2 | async-start | bytes 2097152 | tf_op jit(solution)/shard_map/all_to_all | solution.py:12
  189.4 0.6 eq.15
  190.1 25.4 %all-to-all-done.2 = bf16[16,256,128]{2,1,0:T(8,128)(2,1)S(1)} async-done(((bf16[16,256,128]{2,1,0:T(8,128)(2,1)}), bf16[16,256,128]{2,1,0:T(8,128)(2,1)S(1)}, u32[]{:S(2)}, u32[]{:S(2)}) %all-to-all-start.2) | async-done | bytes 1048608 | tf_op jit(solution)/shard_map/all_to_all | solution.py:12
  215.5 24.0 %gather_fusion = bf16[8192,128]{1,0:T(8,128)(2,1)S(1)} fusion(bf16[4096,128]{1,0:T(8,128)(2,1)S(1)} %bitcast.24, s32[8192]{0:T(1024)S(1)} %fusion.10), kind=kCustom, calls=%fused_computation.1.clone | custom fusion | bytes 4227072 | tf_op jit(solution)/shard_map/jit(_take)/gather | solution.py:107
  239.5 4.3 broadcast_select_fusion
  243.8 1.9 fusion.6
  245.7 9.6 %all-to-all-start.3 = ((bf16[16,256,128]{2,1,0:T(8,128)(2,1)}), bf16[16,256,128]{2,1,0:T(8,128)(2,1)S(1)}, u32[]{:S(2)}, u32[]{:S(2)}) async-start(bf16[16,256,128]{2,1,0:T(8,128)(2,1)} %bitcast.6), calls=%async_computation.3 | async-start | bytes 2097152 | tf_op jit(solution)/shard_map/all_to_all | solution.py:34
  255.3 0.2 convolution_bitcast_fusion
  255.6 0.7 pad_maximum_fusion.1
  256.3 246.6 %all-reduce.2.cloned.1.call-done = f32[33024]{0:T(1024)} async-done(((f32[33024]{0:T(1024)}), f32[33024]{0:T(1024)}) %all-reduce.2.cloned.1.call-update) | async-done | bytes 132112 | tf_op jit(solution)/shard_map/psum | solution.py:52
  502.9 0.9 slice.23
  503.8 0.7 slice.17
  504.5 1.2 slice.24
  505.8 0.1 convert_reduce_fusion.1
  505.9 0.6 add_convert_fusion
  (34 shorter events, 0.6 us)
Async XLA Ops:
  7.2 173.1 %copy-start = (bf16[128,256]{1,0:T(8,128)(2,1)S(1)}, bf16[128,256]{1,0:T(8,128)(2,1)}, u32[]{:S(2)}) copy-start(bf16[128,256]{1,0:T(8,128)(2,1)} %param.12) | copy-start | bytes 196612
  7.2 9.0 %copy-start.4 = (s32[1,16,2,256]{3,2,1,0:T(2,128)S(1)}, s32[1,16,2,256]{3,2,1,0:T(2,128)}, u32[]{:S(2)}) copy-start(s32[1,16,2,256]{3,2,1,0:T(2,128)} %param.10) | copy-start | bytes 98308
  7.2 9.2 %copy-start.3 = (s32[1,16,2,256]{3,2,1,0:T(2,128)S(1)}, s32[1,16,2,256]{3,2,1,0:T(2,128)}, u32[]{:S(2)}) copy-start(s32[1,16,2,256]{3,2,1,0:T(2,128)} %param.11) | copy-start | bytes 98308
  9.3 53.6 %all-to-all-start = ((bf16[16,256,128]{2,1,0:T(8,128)(2,1)}), bf16[16,256,128]{2,1,0:T(8,128)(2,1)S(1)}, u32[]{:S(2)}, u32[]{:S(2)}) async-start(bf16[16,256,128]{2,1,0:T(8,128)(2,1)} %broadcast_in_dim.33), calls=%async_computation | async-start | bytes 2097152 | tf_op jit(solution)/shard_map/all_to_all | solution.py:12
  136.7 1.2 copy-start.1
  140.6 39.5 %copy-start.2 = (bf16[256,128]{1,0:T(8,128)(2,1)S(1)}, bf16[256,128]{1,0:T(8,128)(2,1)}, u32[]{:S(2)}) copy-start(bf16[256,128]{1,0:T(8,128)(2,1)} %param.9) | copy-start | bytes 196612
  140.6 39.6 %copy-start.6 = (f32[256]{0:T(256)S(1)}, f32[256]{0:T(256)}, u32[]{:S(2)}) copy-start(f32[256]{0:T(256)} %param.13) | copy-start | bytes 3076
  140.6 39.2 %all-to-all-start.1 = ((bf16[16,256,129]{1,2,0:T(8,128)(2,1)}), bf16[16,256,129]{1,2,0:T(8,128)(2,1)S(1)}, u32[]{:S(2)}, u32[]{:S(2)}) async-start(bf16[16,256,129]{1,2,0:T(8,128)(2,1)} %copy.16), calls=%async_computation.1 | async-start | bytes 2228224 | tf_op jit(solution)/shard_map/all_to_all | solution.py:34
  183.4 32.0 %all-to-all-start.2 = ((bf16[16,256,128]{2,1,0:T(8,128)(2,1)}), bf16[16,256,128]{2,1,0:T(8,128)(2,1)S(1)}, u32[]{:S(2)}, u32[]{:S(2)}) async-start(bf16[16,256,128]{2,1,0:T(8,128)(2,1)} %broadcast_in_dim.36), calls=%async_computation.2 | async-start | bytes 2097152 | tf_op jit(solution)/shard_map/all_to_all | solution.py:12
  239.5 4.3 copy-start.5
  245.7 260.1 %all-to-all-start.3 = ((bf16[16,256,128]{2,1,0:T(8,128)(2,1)}), bf16[16,256,128]{2,1,0:T(8,128)(2,1)S(1)}, u32[]{:S(2)}, u32[]{:S(2)}) async-start(bf16[16,256,128]{2,1,0:T(8,128)(2,1)} %bitcast.6), calls=%async_computation.3 | async-start | bytes 2097152 | tf_op jit(solution)/shard_map/all_to_all | solution.py:34
  255.3 247.6 %all-reduce.2.cloned.1.call-start = ((), (), s32[]{:S(2)}) async-start(), calls=%async_computation.4 | async-start | bytes 270336 | tf_op jit(solution)/shard_map/psum | solution.py:52
Sparse Core Ops, SparseCore 0:
  261.6 241.2 all-reduce.1
where the time goes:
time: 514 us; the launch traced here: 513 us
  waiting for transfers between devices  300 us (58%)
  other arithmetic  124 us (24%)
  local copies, waits for them, and re-layouts  37.6 us (7%)
  starting transfers between devices  33.1 us (6%)
  between operations  14.3 us (3%)
    psum x1, waiting for transfers between devices, together(): subtotal = lax.psum(jnp.concatenate([a.ravel() for a in arrays]), axis)  247 us
    scatter-add x1, other arithmetic, on_device(): jnp.zeros((panel_rows, feature_width), jnp.float32).at[targets.reshape(-1)]  73.9 us
    scatter-add x1, other arithmetic, on_device(): jnp.zeros((panel_rows,), jnp.float32).at[flat_rows.reshape(-1)].add(1.0)  43.2 us
    all_to_all x2, waiting for transfers between devices, summed_on_arrival(): lax.all_to_all(parts, axis, split_axis=0, concat_axis=0, tiled=True)  27.8 us
    all_to_all x2, waiting for transfers between devices, from_everyone(): return lax.all_to_all(copies, axis, split_axis=0, concat_axis=0, tiled=True)  25.4 us
    gather x1, local copies, waits for them, and re-layouts, on_device(): jnp.take(back_panel, targets.reshape(-1), axis=0)  24 us
    all_to_all x2, starting transfers between devices, summed_on_arrival(): lax.all_to_all(parts, axis, split_axis=0, concat_axis=0, tiled=True)  20.2 us
    all_to_all x2, starting transfers between devices, from_everyone(): return lax.all_to_all(copies, axis, split_axis=0, concat_axis=0, tiled=True)  12.9 us
  transfers between devices with their start and end apart: 5, of which 3 were waited for; matrix products, arithmetic and copies ran while one was open for 10% of the time, Pallas kernels for 0%

commit v1 on v0

--- a/solution.py
+++ b/solution.py
@@ -3,6 +3,7 @@
 import jax.numpy as jnp
 from jax import lax
 from jax.sharding import PartitionSpec as P
+from jax.lax import all_gather
 
 CB = 128
 
@@ -49,7 +50,7 @@
     ends = [0]
     for a in arrays:
         ends.append(ends[-1] + a.size)
-    subtotal = lax.psum(jnp.concatenate([a.ravel() for a in arrays]), axis)
+    subtotal = jnp.sum(all_gather(jnp.concatenate([a.ravel() for a in arrays]), axis), 0)
     return tuple((subtotal[b:e].reshape(a.shape) for a, b, e in zip(arrays, ends, ends[1:])))
 
 

time: 514 us -> 994 us (1.93)
  waiting for transfers between devices: 300 us -> 723 us
  other arithmetic: 124 us -> 161 us
  blocking collectives: 0 us -> 27.6 us
    all_gather x0 -> x1, waiting for transfers between devices: none -> 669 us  [together(): all_gather(jnp.concatenate([a.ravel() for a in arrays]), axis)]
    psum x1 -> x0, waiting for transfers between devices: 247 us -> none  [together(): subtotal = lax.psum(jnp.concatenate([a.ravel() for a in arrays]), axis)]
    reduce_sum x0 -> x1, other arithmetic: none -> 37.5 us  [together(): jnp.sum(all_gather(jnp.concatenate([a.ravel() for a in arrays]), axis), 0)]
    all_to_all x0 -> x1, blocking collectives: none -> 27.6 us  [summed_on_arrival(): lax.all_to_all(parts, axis, split_axis=0, concat_axis=0, tiled=True)]
    all_to_all x2 -> x1, starting transfers between devices: 20.2 us -> 10.6 us  [summed_on_arrival(): lax.all_to_all(parts, axis, split_axis=0, concat_axis=0, tiled=True)]
    all_to_all x2 -> x1, waiting for transfers between devices: 27.8 us -> 27.8 us  [summed_on_arrival(): lax.all_to_all(parts, axis, split_axis=0, concat_axis=0, tiled=True)]
  transfers between devices with their start and end apart: 5 -> 4, of which waited for: 3 -> 3; matrix products, arithmetic and copies ran while one was open for 10% -> 8% of each run, Pallas kernels for 0% -> 0%
where the time goes in v1:
time: 994 us; the launch traced here: 988 us
  waiting for transfers between devices  723 us (73%)
  other arithmetic  161 us (16%)
  local copies, waits for them, and re-layouts  36.1 us (4%)
  blocking collectives  27.6 us (3%)
  starting transfers between devices  23.5 us (2%)
  between operations  14.3 us (1%)
    all_gather x1, waiting for transfers between devices, together(): all_gather(jnp.concatenate([a.ravel() for a in arrays]), axis)  669 us
    scatter-add x1, other arithmetic, on_device(): jnp.zeros((panel_rows, feature_width), jnp.float32).at[targets.reshape(-1)]  73.9 us
    scatter-add x1, other arithmetic, on_device(): jnp.zeros((panel_rows,), jnp.float32).at[flat_rows.reshape(-1)].add(1.0)  43.2 us
    reduce_sum x1, other arithmetic, together(): jnp.sum(all_gather(jnp.concatenate([a.ravel() for a in arrays]), axis), 0)  37.5 us
    all_to_all x1, waiting for transfers between devices, summed_on_arrival(): lax.all_to_all(parts, axis, split_axis=0, concat_axis=0, tiled=True)  27.8 us
    all_to_all x1, blocking collectives, summed_on_arrival(): lax.all_to_all(parts, axis, split_axis=0, concat_axis=0, tiled=True)  27.6 us
    all_to_all x2, waiting for transfers between devices, from_everyone(): return lax.all_to_all(copies, axis, split_axis=0, concat_axis=0, tiled=True)  26 us
    gather x1, local copies, waits for them, and re-layouts, on_device(): jnp.take(back_panel, targets.reshape(-1), axis=0)  24 us
  transfers between devices with their start and end apart: 4, of which 3 were waited for; matrix products, arithmetic and copies ran while one was open for 8% of the time, Pallas kernels for 0%

profile of v1, /device:TPU:1, one launch (start us, length us, event | category | flops | bytes accessed | tf_op | source)
XLA Modules:
  0.0 988.5 jit_solution(3612779532602914927)
XLA Ops:
  7.2 2.1 broadcast_in_dim.33
  9.3 6.9 all-to-all-start
  16.3 43.2 %scatter_custom_fusion.1 = f32[4096]{0:T(1024)S(1)} fusion(s32[8192]{0:T(1024)S(1)} %bitcast.38, f32[8192]{0:T(1024)S(1)} %broadcast.37, f32[]{:T(128)} %constant.15.clone.1), kind=kCustom, calls=%fused_computation.37 | custom fusion | flops 8192 | bytes 16388 | tf_op jit(solution)/shard_map/scatter-add | solution.py:80
  59.6 3.1 concatenate.15
  62.9 73.9 %scatter_custom_fusion = f32[4096,128]{1,0:T(8,128)S(1)} fusion(s32[8192]{0:T(1024)S(1)} %bitcast.39, pred[8192]{0:T(1024)(128)(4,1)S(1)} %compare_and_fusion.1, bf16[]{:T(256)} %constant.11.clone.2, f32[]{:T(128)} %constant.15.clone.1, bf16[4096,128]{1,0:T(8,128)(2,1)S(1)} %bitcast.25, s32[8192]{0:T(1024)S(1)} %broadcast_clamp_fusion), kind=kCustom, calls=%fused_computation.5 | custom fusion | flops 3145728 | bytes 3186694 | tf_op jit(solution)/shard_map/scatter-add | solution.py:88
  136.8 0.1 convert_element_type.55
  136.9 1.1 copy-done.1
  138.0 0.5 pad_maximum_fusion
  138.5 2.1 copy.16
  140.6 10.6 %all-to-all-start.1 = ((bf16[16,256,129]{1,2,0:T(8,128)(2,1)}), bf16[16,256,129]{1,2,0:T(8,128)(2,1)S(1)}, u32[]{:S(2)}, u32[]{:S(2)}) async-start(bf16[16,256,129]{1,2,0:T(8,128)(2,1)} %copy.16), calls=%async_computation.1 | async-start | bytes 2228224 | tf_op jit(solution)/shard_map/all_to_all | solution.py:35
  151.2 0.8 dynamic-slice_convert_fusion
  152.0 27.8 %all-to-all-done.1 = bf16[16,256,129]{1,2,0:T(8,128)(2,1)S(1)} async-done(((bf16[16,256,129]{1,2,0:T(8,128)(2,1)}), bf16[16,256,129]{1,2,0:T(8,128)(2,1)S(1)}, u32[]{:S(2)}, u32[]{:S(2)}) %all-to-all-start.1) | async-done | bytes 1056800 | tf_op jit(solution)/shard_map/all_to_all | solution.py:35
  179.8 0.2 convert_reduce_fusion
  180.0 0.1 copy.18
  180.1 0.1 divide_convert_fusion
  180.2 1.8 convert_reduce_fusion.2
  182.1 0.2 convolution_bitcast_fusion
  182.4 0.8 reshape.125
  183.1 0.2 fusion.7
  183.3 1.2 broadcast_in_dim.36
  184.5 6.0 all-to-all-start.2
  190.6 26.0 %all-to-all-done.2 = bf16[16,256,128]{2,1,0:T(8,128)(2,1)S(1)} async-done(((bf16[16,256,128]{2,1,0:T(8,128)(2,1)}), bf16[16,256,128]{2,1,0:T(8,128)(2,1)S(1)}, u32[]{:S(2)}, u32[]{:S(2)}) %all-to-all-start.2) | async-done | bytes 1048608 | tf_op jit(solution)/shard_map/all_to_all | solution.py:13
  216.6 24.0 %gather_fusion = bf16[8192,128]{1,0:T(8,128)(2,1)S(1)} fusion(bf16[4096,128]{1,0:T(8,128)(2,1)S(1)} %bitcast.24, s32[8192]{0:T(1024)S(1)} %fusion.10), kind=kCustom, calls=%fused_computation.1.clone | custom fusion | bytes 4227072 | tf_op jit(solution)/shard_map/jit(_take)/gather | solution.py:108
  240.6 4.3 broadcast_select_fusion
  244.9 0.9 fusion.6
  245.8 27.6 %all_to_all.20 = bf16[16,256,128]{2,1,0:T(8,128)(2,1)S(1)} all-to-all(bf16[16,256,128]{2,1,0:T(8,128)(2,1)S(1)} %bitcast.28), channel_id=1, replica_groups=mesh['blk'=16,'rep'=16] {'blk'}, dimensions={0} | all-to-all | bytes 2097152 | tf_op jit(solution)/shard_map/all_to_all | solution.py:35
  273.3 0.1 convert_reduce_fusion.1
  273.5 0.6 add_convert_fusion
  274.1 668.8 %all-gather.4.cloned.1.call-done = f32[256,1,33024]{2,1,0:T(1,128)} async-done(((f32[1,1,33024]{2,1,0:T(1,128)}), f32[256,1,33024]{2,1,0:T(1,128)}) %all-gather.4.cloned.1.call-update) | async-done | bytes 33816592 | tf_op jit(solution)/shard_map/all_gather | solution.py:53
  942.9 37.5 %reduce_sum.39 = f32[33024]{0:T(1024)S(1)} reduce(f32[256,1,33024]{2,1,0:T(1,128)} %all-gather.4.cloned.1.call-done, f32[]{:T(128)} %constant.15.clone.1), dimensions={0,1}, to_apply=%region_5.7 | reduce | flops 8421120 | bytes 33948676 | tf_op jit(solution)/shard_map/reduce_sum | solution.py:53
  980.4 0.6 slice.24
  980.9 0.7 slice.17
  (33 shorter events, 0.5 us)
Async XLA Ops:
  7.2 173.1 %copy-start = (bf16[128,256]{1,0:T(8,128)(2,1)S(1)}, bf16[128,256]{1,0:T(8,128)(2,1)}, u32[]{:S(2)}) copy-start(bf16[128,256]{1,0:T(8,128)(2,1)} %param.12) | copy-start | bytes 196612
  7.2 9.0 copy-start.4
  7.2 55.6 %copy-start.3 = (s32[1,16,2,256]{3,2,1,0:T(2,128)S(1)}, s32[1,16,2,256]{3,2,1,0:T(2,128)}, u32[]{:S(2)}) copy-start(s32[1,16,2,256]{3,2,1,0:T(2,128)} %param.11) | copy-start | bytes 98308
  9.3 53.6 %all-to-all-start = ((bf16[16,256,128]{2,1,0:T(8,128)(2,1)}), bf16[16,256,128]{2,1,0:T(8,128)(2,1)S(1)}, u32[]{:S(2)}, u32[]{:S(2)}) async-start(bf16[16,256,128]{2,1,0:T(8,128)(2,1)} %broadcast_in_dim.33), calls=%async_computation | async-start | bytes 2097152 | tf_op jit(solution)/shard_map/all_to_all | solution.py:13
  136.8 1.2 copy-start.1
  140.6 39.5 %copy-start.2 = (bf16[256,128]{1,0:T(8,128)(2,1)S(1)}, bf16[256,128]{1,0:T(8,128)(2,1)}, u32[]{:S(2)}) copy-start(bf16[256,128]{1,0:T(8,128)(2,1)} %param.9) | copy-start | bytes 196612
  140.6 39.6 %copy-start.5 = (f32[256]{0:T(256)S(1)}, f32[256]{0:T(256)}, u32[]{:S(2)}) copy-start(f32[256]{0:T(256)} %param.13) | copy-start | bytes 3076
  140.6 39.2 %all-to-all-start.1 = ((bf16[16,256,129]{1,2,0:T(8,128)(2,1)}), bf16[16,256,129]{1,2,0:T(8,128)(2,1)S(1)}, u32[]{:S(2)}, u32[]{:S(2)}) async-start(bf16[16,256,129]{1,2,0:T(8,128)(2,1)} %copy.16), calls=%async_computation.1 | async-start | bytes 2228224 | tf_op jit(solution)/shard_map/all_to_all | solution.py:35
  151.2 791.7 %all-gather.4.cloned.1.call-start = ((), (), s32[]{:S(2)}) async-start(), calls=%async_computation.4 | async-start | bytes 33948672 | tf_op jit(solution)/shard_map/all_gather | solution.py:53
  184.5 32.0 %all-to-all-start.2 = ((bf16[16,256,128]{2,1,0:T(8,128)(2,1)}), bf16[16,256,128]{2,1,0:T(8,128)(2,1)S(1)}, u32[]{:S(2)}, u32[]{:S(2)}) async-start(bf16[16,256,128]{2,1,0:T(8,128)(2,1)} %broadcast_in_dim.36), calls=%async_computation.2 | async-start | bytes 2097152 | tf_op jit(solution)/shard_map/all_to_all | solution.py:13
Sparse Core Ops, SparseCore 0:
  183.3 759.5 all-gather.3
